TPU v7x, 32 devices: a whole 2x2x4 slice. The times are simulated.
32 devices in a mesh: grp: 2 (over y), sink: 16 (over z, x, core).
Axes of the slice: x: 2, y: 2, z: 4, core: 2. Of those that a mesh axis runs over, the one named last changes fastest.
Arguments:
- meson: float32 [32, 2, 256, 256], P(('grp', 'sink')), parts along dimension 0, may hold values from -0.25 to 0.25
- meson_src: float32 [8192, 256], P(('grp', 'sink')), parts along dimension 0, may hold values from -0.25 to 0.25
- peram: float32 [32, 8, 2, 256, 256], P(('grp', 'sink')), parts along dimension 0, may hold values from -0.375 to 0.375
- pair_left: int32 [32, 16], P(('grp', 'sink')), parts along dimension 0, may hold values from 0 to 7
- pair_right: int32 [32, 16], P(('grp', 'sink')), parts along dimension 0, may hold values from 0 to 7
- pair_weight: int32 [32, 16], P(('grp', 'sink')), parts along dimension 0, may hold values from -2 to 2
- pair_count: int32 [32], P(('grp', 'sink')), parts along dimension 0, may hold values from 1 to 16, 136 in all
Outputs:
- two_meson: float32 [32, 2, 256, 256], P(('grp', 'sink')), parts along dimension 0
There are 2 independent parts, one for each index of `grp`. A program takes and returns all parts, laid end to end along the dimension named above; each array names one. Nothing has to cross between parts.
Inputs may be any that keep to these rules, and one draw needn't show every extreme that they name: `pair_count`: each sink time's count is at least 1 and some sink time has exactly 16; entries past the count are ignored.
All inputs are finite; a program needn't handle non-finite values. No bound on the sum of `pair_count` on one device may be relied on, other than what follows from the above.
Results may differ from a plain program's by a relative error of at most 0.0003.
Values sent between devices are 32-bit elements; how exact they have to be, the bound alone decides.
No kernel may reach another device: no remote copies, remote signals or barrier semaphores. Data moves between devices by JAX's collectives and lax.ppermute only.
A program may use at most 64 MiB of HBM per device.

v0:
```python
from functools import partial

import jax
import jax.numpy as jnp
from jax import lax
from jax.experimental import pallas as pl
from jax.experimental.pallas import tpu as pltpu
from jax.sharding import PartitionSpec as P

F32 = jnp.float32
NN = (((1,), (0,)), ((), ()))
NT = (((1,), (1,)), ((), ()))
ROWS = (64, 64, 64, 64)


def swapped(value, axis, mask):
    pairs = [(source, source ^ mask) for source in range(lax.axis_size(axis))]
    return lax.ppermute(value, axis, pairs)


def sent(value, axis, mask, senders):
    return lax.ppermute(value, axis, [(source, source ^ mask) for source in senders])


def halves(value):
    high = value.astype(jnp.bfloat16)
    return high, (value - high.astype(F32)).astype(jnp.bfloat16)


def product(left, right, adjoint=False):
    (rh, rl), (ih, il) = halves(left[0]), halves(left[1])
    left_terms = jnp.concatenate([rh, ih, rh, ih, rl, il], axis=1)
    (rh, rl), (ih, il) = halves(right[0]), halves(right[1])
    if adjoint:
        real = jnp.concatenate([rh, ih, rl, il, rh, ih], axis=1)
        imag = jnp.concatenate([-ih, rh, -il, rl, -ih, rh], axis=1)
    else:
        real = jnp.concatenate([rh, -ih, rl, -il, rh, -ih], axis=0)
        imag = jnp.concatenate([ih, rh, il, rl, ih, rh], axis=0)
    dot = partial(
        lax.dot_general,
        left_terms,
        dimension_numbers=NT if adjoint else NN,
        preferred_element_type=F32,
    )
    return dot(real), dot(imag)


def block_kernel(spans, place, meson, tau, first, second, *refs):
    chunks, blocks = refs[-1 - len(spans) : -1], refs[-1]
    odd = place[1] == 1
    one, two = first[0], second[0]
    source = (jnp.where(odd, two, one), jnp.where(odd, one, two))
    wave = (tau[0, 0, 0], tau[0, 0, 1])
    hold = product(source, wave, adjoint=True)
    front = product((meson[0, 0], meson[0, 1]), wave)
    block = product(front, hold)
    for part in range(2):
        blocks[0, part] = block[part]
        for (low, size), chunk in zip(spans, chunks, strict=True):
            chunk[0, part] = block[part][low : low + size]


def blocks_of(place, meson, peram, first, second, blocks, start, spans):
    size, width = first.shape[0], first.shape[-1]
    sources = peram.shape[1]
    whole = (1, 2, width, width)
    in_specs = [
        pl.BlockSpec(whole, lambda i, p: (0, 0, 0, 0)),
        pl.BlockSpec((1,) + whole, lambda i, p: (0, p[0] ^ (start + i), 0, 0, 0)),
        pl.BlockSpec((1, width, width), lambda i, p: (i, 0, 0)),
        pl.BlockSpec((1, width, width), lambda i, p: (i, 0, 0)),
    ]
    operands = [meson, peram, first, second]
    aliases = {}
    if blocks is not None:
        in_specs.append(pl.BlockSpec(memory_space=pl.ANY))
        operands.append(blocks)
        aliases = {len(operands): len(spans)}
    shapes = [jax.ShapeDtypeStruct((size, 2, rows, width), F32) for _, rows in spans]
    shapes.append(jax.ShapeDtypeStruct((sources, 2, width, width), F32))
    out_specs = [pl.BlockSpec((1, 2, rows, width), lambda i, p: (i, 0, 0, 0)) for _, rows in spans]
    out_specs.append(pl.BlockSpec(whole, lambda i, p: (start + i, 0, 0, 0)))
    outs = pl.pallas_call(
        partial(block_kernel, spans),
        out_shape=shapes,
        grid_spec=pltpu.PrefetchScalarGridSpec(
            num_scalar_prefetch=1, grid=(size,), in_specs=in_specs, out_specs=out_specs
        ),
        input_output_aliases=aliases,
        cost_estimate=pl.CostEstimate(
            flops=size * 72 * width**3, bytes_accessed=size * 28 * width**2, transcendentals=0
        ),
        name="blocks",
    )(place, *operands)
    return outs[:-1], outs[-1]


def mix_kernel(own_list, other_list, place, blocks, left, right):
    left[...] = jnp.zeros_like(left)
    right[...] = jnp.zeros_like(right)
    here, there = place[0], place[2]

    def own(e, _):
        weight = own_list[2, e].astype(F32)
        left[own_list[1, e] ^ there] += weight * blocks[own_list[0, e] ^ here]
        return 0

    def other(e, _):
        weight = other_list[2, e].astype(F32)
        right[other_list[0, e] ^ there] += weight * blocks[other_list[1, e] ^ here]
        return 0

    lax.fori_loop(0, own_list[3, 0], own, 0)
    lax.fori_loop(0, other_list[3, 0], other, 0)


def mixed(own_list, other_list, place, blocks):
    smem, vmem = pl.BlockSpec(memory_space=pltpu.SMEM), pl.BlockSpec(memory_space=pltpu.VMEM)
    shape = jax.ShapeDtypeStruct(blocks.shape, F32)
    return pl.pallas_call(
        mix_kernel,
        out_shape=(shape, shape),
        in_specs=[smem, smem, smem, vmem],
        out_specs=(vmem, vmem),
        cost_estimate=pl.CostEstimate(
            flops=blocks.size * 4, bytes_accessed=blocks.size * 12, transcendentals=0
        ),
        name="mix",
    )(own_list, other_list, place, blocks)


def finish_kernel(chunk, left, right, *refs):
    result, back = refs[-2:]
    block = (chunk[0, 0], chunk[0, 1])
    forth = product((left[0, 0], left[0, 1]), block)
    home = product(block, (right[0, 0], right[0, 1]))

    @pl.when(pl.program_id(0) == 0)
    def _():
        for part in range(2):
            if len(refs) == 4:
                result[part] = refs[0][part]
                back[part] = refs[1][part]
            else:
                result[part] = jnp.zeros_like(result[part])
                back[part] = jnp.zeros_like(back[part])

    for part in range(2):
        result[part] += forth[part]
        back[part] += home[part]


def finished(chunk, left, right, start, sums):
    size, width = chunk.shape[0], chunk.shape[-1]
    whole = (1, 2, width, width)
    total = pl.BlockSpec((2, width, width), lambda i: (0, 0, 0))
    shape = jax.ShapeDtypeStruct((2, width, width), F32)
    return pl.pallas_call(
        finish_kernel,
        out_shape=(shape, shape),
        grid=(size,),
        in_specs=[
            pl.BlockSpec(whole, lambda i: (i, 0, 0, 0)),
            pl.BlockSpec(whole, lambda i: (start + i, 0, 0, 0)),
            pl.BlockSpec(whole, lambda i: (start + i, 0, 0, 0)),
        ]
        + [total] * len(sums),
        out_specs=(total, total),
        cost_estimate=pl.CostEstimate(
            flops=size * 48 * width**3, bytes_accessed=size * 24 * width**2, transcendentals=0
        ),
        name="finish",
    )(chunk, left, right, *sums)


def back_kernel(low, size, chunk, right, back, out):
    real, imag = back[0, low : low + size], back[1, low : low + size]
    for k in range(chunk.shape[0]):
        more = product((chunk[k, 0], chunk[k, 1]), (right[k, 0], right[k, 1]))
        real += more[0]
        imag += more[1]
    out[0], out[1] = real, imag


def rows_back(chunk, right, start, back, low):
    size, _, rows, width = chunk.shape
    return pl.pallas_call(
        partial(back_kernel, low, rows),
        out_shape=jax.ShapeDtypeStruct((2, rows, width), F32),
        grid=(1,),
        in_specs=[
            pl.BlockSpec(chunk.shape, lambda i: (0, 0, 0, 0)),
            pl.BlockSpec((size, 2, width, width), lambda i: (start // size, 0, 0, 0)),
            pl.BlockSpec(back.shape, lambda i: (0, 0, 0)),
        ],
        out_specs=pl.BlockSpec((2, rows, width), lambda i: (0, 0, 0)),
        cost_estimate=pl.CostEstimate(
            flops=size * 24 * rows * width**2, bytes_accessed=12 * width**2, transcendentals=0
        ),
        name="rows_back",
    )(chunk, right, back)


def last_kernel(spans, left, result, *refs):
    chunks, out = refs[:-1], refs[-1]
    real, imag = result[0], result[1]
    for k in range(left.shape[0]):
        block = tuple(jnp.concatenate([chunk[k, part] for chunk in chunks]) for part in range(2))
        more = product((left[k, 0], left[k, 1]), block)
        real += more[0]
        imag += more[1]
    out[0], out[1] = real, imag


def last_added(chunks, left, start, result, spans):
    size, width = chunks[0].shape[0], chunks[0].shape[-1]
    return pl.pallas_call(
        partial(last_kernel, spans),
        out_shape=jax.ShapeDtypeStruct(result.shape, F32),
        grid=(1,),
        in_specs=[
            pl.BlockSpec((size, 2, width, width), lambda i: (start // size, 0, 0, 0)),
            pl.BlockSpec(result.shape, lambda i: (0, 0, 0)),
        ]
        + [pl.BlockSpec(chunk.shape, lambda i: (0, 0, 0, 0)) for chunk in chunks],
        out_specs=pl.BlockSpec(result.shape, lambda i: (0, 0, 0)),
        cost_estimate=pl.CostEstimate(
            flops=size * 24 * width**3, bytes_accessed=24 * width**2, transcendentals=0
        ),
        name="last",
    )(left, result, *chunks)


def body(meson, meson_src, peram, pair_left, pair_right, pair_weight, pair_count):
    axis = "sink"
    n = lax.axis_size(axis)
    sources, width = peram.shape[1], peram.shape[3]
    group, half = n // sources, n // 2
    me = lax.axis_index(axis)
    senders = [d for d in range(n) if (d & 1) == d // half]
    receivers = [d ^ half for d in senders]
    is_sender = (me & 1) == me // half
    mine = me // group

    def whole(shards):
        if group == 2:
            return shards, swapped(shards, axis, 1)
        for bit in range(group.bit_length() - 1):
            other = swapped(shards, axis, 1 << bit)
            upper = ((me >> bit) & 1) == 1
            low, high = jnp.where(upper, other, shards), jnp.where(upper, shards, other)
            shards = jnp.concatenate([low, high], axis=1)
        return shards[:, :width], shards[:, width:]

    odd = me & 1 if group == 2 else 0
    place = jnp.stack([mine, odd, mine ^ (sources // 2)]).astype(jnp.int32)
    count = jnp.broadcast_to(pair_count[:, None], pair_left.shape)
    own_list = jnp.concatenate([pair_left, pair_right, pair_weight, count])

    w0 = meson_src[None]
    s0 = whole(w0)
    w4 = swapped(w0, axis, half)
    w1 = swapped(w0, axis, group)
    s1 = whole(w1)
    w23 = swapped(jnp.concatenate([w0, w1]), axis, 2 * group)
    s23 = whole(w23)
    w45 = jnp.concatenate([w4, swapped(w4, axis, group)])
    s45 = whole(w45)
    s67 = whole(swapped(w45, axis, 2 * group))
    other_list = swapped(own_list, axis, half)

    lows = [sum(ROWS[:r]) * width // 256 for r in range(len(ROWS))]
    spans = [(low, rows * width // 256) for low, rows in zip(lows, ROWS, strict=True)]
    blocks, arrived, start = None, [], 0
    for source in (s0, s1, s23, s45):
        (chunk,), blocks = blocks_of(place, meson, peram, *source, blocks, start, [(0, width)])
        arrived.append((start, sent(chunk, axis, half, senders)))
        start += source[0].shape[0]
    chunks, blocks = blocks_of(place, meson, peram, *s67, blocks, start, spans)
    chunks = [sent(chunk, axis, half, senders) for chunk in chunks]

    left, right = mixed(own_list, other_list, place, blocks)
    sums = ()
    for at, chunk in arrived:
        sums = finished(chunk, left, right, at, sums)
    result, back = sums
    returned = [
        sent(rows_back(chunk, right, start, back, low), axis, half, receivers)
        for chunk, (low, _) in zip(chunks, spans, strict=True)
    ]
    result = last_added(chunks, left, start, result, spans)
    return jnp.where(is_sender, jnp.concatenate(returned, axis=1), result)[None]


def solution(mesh):
    placed = (
        P(("grp", "sink"), None, None, None),
        P(("grp", "sink"), None),
        P(("grp", "sink"), None, None, None, None),
        P(("grp", "sink"), None),
        P(("grp", "sink"), None),
        P(("grp", "sink"), None),
        P(("grp", "sink")),
    )
    return jax.shard_map(
        body,
        mesh=mesh,
        in_specs=placed,
        out_specs=P(("grp", "sink"), None, None, None),
        check_vma=False,
    )
```

profile of v0, /device:TPU:8, one launch (start us, length us, event | category | flops | bytes accessed | tf_op | source)
XLA Modules:
  0.0 193.6 jit_solution(1872610643308636667)
XLA Ops:
  0.0 1.5 collective-permute-start.5
  1.5 2.6 %collective-permute-start = (f32[1,256,256]{2,1,0:T(8,128)}, f32[1,256,256]{2,1,0:T(8,128)S(1)}, u32[]{:S(2)}, u32[]{:S(2)}) collective-permute-start(f32[1,256,256]{2,1,0:T(8,128)} %bitcast.8), channel_id=1, source_target_pairs={{0,8},{1,9},{2,10},{3,11},{4,12},{5,13},{6,14},{7,15},{8,0},{9,1},... | collective-permute-start | bytes 786440 | tf_op jit(solution)/shard_map/ppermute | solution.py:18
  4.1 4.2 %collective-permute-done.5.first = f32[1,256,256]{2,1,0:T(8,128)S(1)} collective-permute-done((f32[1,256,256]{2,1,0:T(8,128)}, f32[1,256,256]{2,1,0:T(8,128)S(1)}, u32[]{:S(2)}, u32[]{:S(2)}) %collective-permute-start.5) | collective-permute-done | bytes 262176 | tf_op jit(solution)/shard_map/ppermute | solution.py:18
  9.6 5.6 %collective-permute-done = f32[1,256,256]{2,1,0:T(8,128)S(1)} collective-permute-done((f32[1,256,256]{2,1,0:T(8,128)}, f32[1,256,256]{2,1,0:T(8,128)S(1)}, u32[]{:S(2)}, u32[]{:S(2)}) %collective-permute-start) | collective-permute-done | bytes 262176 | tf_op jit(solution)/shard_map/ppermute | solution.py:18
  15.8 7.7 %collective-permute-done.1 = f32[1,256,256]{2,1,0:T(8,128)S(1)} collective-permute-done((f32[1,256,256]{2,1,0:T(8,128)S(1)}, f32[1,256,256]{2,1,0:T(8,128)S(1)}, u32[]{:S(2)}, u32[]{:S(2)}) %collective-permute-start.1) | collective-permute-done | bytes 262176 | tf_op jit(solution)/shard_map/ppermute | solution.py:18
  23.8 1.5 collective-permute-done.6.first
  28.3 4.5 %blocks.5 = (f32[1,2,256,256]{3,2,1,0:T(8,128)}, f32[8,2,256,256]{3,2,1,0:T(8,128)}) custom-call(s32[3]{0:T(128)} %pad_add_fusion.place, f32[1,2,256,256]{3,2,1,0:T(8,128)} %meson.9, f32[1,8,2,256,256]{4,3,2,1,0:T(8,128)} %tau.9, f32[1,256,256]{2,1,0:T(8,128)} %bitcast.11, f32[1,256,256]{2,1,0:T(8,128)} %copy-done.13), custom_call_target="tpu_custom_call" | custom-call | flops 1207959552 | bytes 1835008 | tf_op jit(solution)/shard_map/blocks/pallas_call | solution.py:84
  33.5 4.5 %blocks.6 = (f32[1,2,256,256]{3,2,1,0:T(8,128)}, f32[8,2,256,256]{3,2,1,0:T(8,128)}) custom-call(s32[3]{0:T(128)} %pad_add_fusion.place, f32[1,2,256,256]{3,2,1,0:T(8,128)} %meson.9, f32[1,8,2,256,256]{4,3,2,1,0:T(8,128)} %tau.9, f32[1,256,256]{2,1,0:T(8,128)} %copy-done.7, f32[1,256,256]{2,1,0:T(8,128)} %copy-done.12, ...), custom_call_target="tpu_custom_call", output_to_operand_aliasing={{1}: (5, {})} | custom-call | flops 1207959552 | bytes 1835008 | tf_op jit(solution)/shard_map/blocks/pallas_call | solution.py:84
  39.1 6.2 %blocks.7 = (f32[2,2,256,256]{3,2,1,0:T(8,128)}, f32[8,2,256,256]{3,2,1,0:T(8,128)}) custom-call(s32[3]{0:T(128)} %pad_add_fusion.place, f32[1,2,256,256]{3,2,1,0:T(8,128)} %meson.9, f32[1,8,2,256,256]{4,3,2,1,0:T(8,128)} %tau.9, f32[2,256,256]{2,1,0:T(8,128)} %copy-done.9, f32[2,256,256]{2,1,0:T(8,128)} %copy-done.10, ...), custom_call_target="tpu_custom_call", output_to_operand_aliasing={{1}: (5, {})} | custom-call | flops 2415919104 | bytes 3670016 | tf_op jit(solution)/shard_map/blocks/pallas_call | solution.py:84
  45.2 6.4 %collective-permute-start.13 = (f32[2,2,256,256]{3,2,1,0:T(8,128)}, f32[2,2,256,256]{3,2,1,0:T(8,128)S(1)}, u32[]{:S(2)}, u32[]{:S(2)}) collective-permute-start(f32[2,2,256,256]{3,2,1,0:T(8,128)} %get-tuple-element.37), channel_id=1, source_target_pairs={{0,8},{2,10},{4,12},{6,14},{9,1},{11,3},{13,5},{15,7},{16,24},{18,... | collective-permute-start | bytes 3145736 | tf_op jit(solution)/shard_map/ppermute | solution.py:22
  52.5 6.3 %blocks.8 = (f32[2,2,256,256]{3,2,1,0:T(8,128)}, f32[8,2,256,256]{3,2,1,0:T(8,128)}) custom-call(s32[3]{0:T(128)} %pad_add_fusion.place, f32[1,2,256,256]{3,2,1,0:T(8,128)} %meson.9, f32[1,8,2,256,256]{4,3,2,1,0:T(8,128)} %tau.9, f32[2,256,256]{2,1,0:T(8,128)} %copy-done, f32[2,256,256]{2,1,0:T(8,128)} %copy-done.11, ...), custom_call_target="tpu_custom_call", output_to_operand_aliasing={{1}: (5, {})} | custom-call | flops 2415919104 | bytes 3670016 | tf_op jit(solution)/shard_map/blocks/pallas_call | solution.py:84
  58.8 1.3 collective-permute-start.12
  60.2 2.1 %collective-permute-start.15 = (f32[1,2,256,256]{3,2,1,0:T(8,128)}, f32[1,2,256,256]{3,2,1,0:T(8,128)}, u32[]{:S(2)}, u32[]{:S(2)}) collective-permute-start(f32[1,2,256,256]{3,2,1,0:T(8,128)} %get-tuple-element.39), channel_id=1, source_target_pairs={{0,8},{2,10},{4,12},{6,14},{9,1},{11,3},{13,5},{15,7},{16,24},{18,... | collective-permute-start | bytes 1572872 | tf_op jit(solution)/shard_map/ppermute | solution.py:22
  63.0 2.1 %collective-permute-start.14 = (f32[1,2,256,256]{3,2,1,0:T(8,128)}, f32[1,2,256,256]{3,2,1,0:T(8,128)}, u32[]{:S(2)}, u32[]{:S(2)}) collective-permute-start(f32[1,2,256,256]{3,2,1,0:T(8,128)} %get-tuple-element.38), channel_id=1, source_target_pairs={{0,8},{2,10},{4,12},{6,14},{9,1},{11,3},{13,5},{15,7},{16,24},{18,... | collective-permute-start | bytes 1572872 | tf_op jit(solution)/shard_map/ppermute | solution.py:22
  65.2 6.2 %blocks.9 = (f32[2,2,64,256]{3,2,1,0:T(8,128)}, f32[2,2,64,256]{3,2,1,0:T(8,128)}, f32[2,2,64,256]{3,2,1,0:T(8,128)}, f32[2,2,64,256]{3,2,1,0:T(8,128)}, f32[8,2,256,256]{3,2,1,0:T(8,128)}) custom-call(s32[3]{0:T(128)} %pad_add_fusion.place, f32[1,2,256,256]{3,2,1,0:T(8,128)} %meson.9, f32[1,8,2,256,256]{4,3,2,1,0:T(8,128)} %tau.9, ...), custom_call_target="tpu_custom_call", output_to_operand_aliasing={{4}: (5, {})} | custom-call | flops 2415919104 | bytes 3670016 | tf_op jit(solution)/shard_map/blocks/pallas_call | solution.py:84
  71.5 62.0 %collective-permute-done.11.other_list = s32[4,16]{1,0:T(4,128)S(1)} collective-permute-done((s32[4,16]{1,0:T(4,128)S(1)}, s32[4,16]{1,0:T(4,128)S(1)}, u32[]{:S(2)}, u32[]{:S(2)}) %collective-permute-start.11) | collective-permute-done | bytes 288 | tf_op jit(solution)/shard_map/ppermute | solution.py:18
  133.4 5.3 %collective-permute-start.10 = (f32[2,2,64,256]{3,2,1,0:T(8,128)}, f32[2,2,64,256]{3,2,1,0:T(8,128)S(1)}, u32[]{:S(2)}, u32[]{:S(2)}) collective-permute-start(f32[2,2,64,256]{3,2,1,0:T(8,128)} %get-tuple-element.32), channel_id=1, source_target_pairs={{0,8},{2,10},{4,12},{6,14},{9,1},{11,3},{13,5},{15,7},{16,24},{18,... | collective-permute-start | bytes 786440 | tf_op jit(solution)/shard_map/ppermute | solution.py:22
  138.7 6.3 %mix.1 = (f32[8,2,256,256]{3,2,1,0:T(8,128)}, f32[8,2,256,256]{3,2,1,0:T(8,128)}) custom-call(s32[4,16]{1,0:T(4,128)} %copy-done.14, s32[4,16]{1,0:T(4,128)} %copy-done.15, s32[3]{0:T(128)} %pad_add_fusion.place, f32[8,2,256,256]{3,2,1,0:T(8,128)} %get-tuple-element.33.blocks), custom_call_target="tpu_custom_call" | custom-call | flops 4194304 | bytes 12582912 | tf_op jit(solution)/shard_map/mix/pallas_call | solution.py:121
  145.1 1.3 collective-permute-start.17
  146.4 3.2 %finish.4 = (f32[2,256,256]{2,1,0:T(8,128)}, f32[2,256,256]{2,1,0:T(8,128)}) custom-call(f32[1,2,256,256]{3,2,1,0:T(8,128)} %collective-permute-done.15.chunk, f32[8,2,256,256]{3,2,1,0:T(8,128)} %get-tuple-element.36.left, f32[8,2,256,256]{3,2,1,0:T(8,128)} %get-tuple-element.34.right), custom_call_target="tpu_custom_call" | custom-call | flops 805306368 | bytes 1572864 | tf_op jit(solution)/shard_map/finish/pallas_call | solution.py:159
  149.6 1.3 collective-permute-start.19
  150.9 3.5 %finish.5 = (f32[2,256,256]{2,1,0:T(8,128)}, f32[2,256,256]{2,1,0:T(8,128)}) custom-call(f32[1,2,256,256]{3,2,1,0:T(8,128)} %collective-permute-done.14.chunk, f32[8,2,256,256]{3,2,1,0:T(8,128)} %get-tuple-element.36.left, f32[8,2,256,256]{3,2,1,0:T(8,128)} %get-tuple-element.34.right, f32[2,256,256]{2,1,0:T(8,128)} %get-tuple-element.40.refs_0_, ...), custom_call_target="tpu_custom_call" | custom-call | flops 805306368 | bytes 1572864 | tf_op jit(solution)/shard_map/finish/pallas_call | solution.py:159
  154.4 1.5 collective-permute-start.21
  155.9 5.1 %finish.6 = (f32[2,256,256]{2,1,0:T(8,128)}, f32[2,256,256]{2,1,0:T(8,128)}) custom-call(f32[2,2,256,256]{3,2,1,0:T(8,128)} %copy-done.1, f32[8,2,256,256]{3,2,1,0:T(8,128)} %get-tuple-element.36.left, f32[8,2,256,256]{3,2,1,0:T(8,128)} %get-tuple-element.34.right, f32[2,256,256]{2,1,0:T(8,128)} %get-tuple-element.42.refs_0_, ...), custom_call_target="tpu_custom_call" | custom-call | flops 1610612736 | bytes 3145728 | tf_op jit(solution)/shard_map/finish/pallas_call | solution.py:159
  161.9 5.0 %finish.7 = (f32[2,256,256]{2,1,0:T(8,128)}, f32[2,256,256]{2,1,0:T(8,128)}) custom-call(f32[2,2,256,256]{3,2,1,0:T(8,128)} %copy-done.2, f32[8,2,256,256]{3,2,1,0:T(8,128)} %get-tuple-element.36.left, f32[8,2,256,256]{3,2,1,0:T(8,128)} %get-tuple-element.34.right, f32[2,256,256]{2,1,0:T(8,128)} %get-tuple-element.44.refs_0_, ...), custom_call_target="tpu_custom_call" | custom-call | flops 1610612736 | bytes 3145728 | tf_op jit(solution)/shard_map/finish/pallas_call | solution.py:159
  167.7 2.8 %rows_back.4 = f32[2,64,256]{2,1,0:T(8,128)} custom-call(f32[2,2,64,256]{3,2,1,0:T(8,128)} %copy-done.3, f32[8,2,256,256]{3,2,1,0:T(8,128)} %get-tuple-element.34.right, f32[2,256,256]{2,1,0:T(8,128)} %get-tuple-element.46.back), custom_call_target="tpu_custom_call" | custom-call | flops 201326592 | bytes 786432 | tf_op jit(solution)/shard_map/rows_back/pallas_call | solution.py:188
  170.5 1.3 collective-permute-start.16
  172.5 2.8 %rows_back.5 = f32[2,64,256]{2,1,0:T(8,128)} custom-call(f32[2,2,64,256]{3,2,1,0:T(8,128)} %copy-done.4, f32[8,2,256,256]{3,2,1,0:T(8,128)} %get-tuple-element.34.right, f32[2,256,256]{2,1,0:T(8,128)} %get-tuple-element.46.back), custom_call_target="tpu_custom_call" | custom-call | flops 201326592 | bytes 786432 | tf_op jit(solution)/shard_map/rows_back/pallas_call | solution.py:188
  177.2 2.8 %rows_back.6 = f32[2,64,256]{2,1,0:T(8,128)} custom-call(f32[2,2,64,256]{3,2,1,0:T(8,128)} %copy-done.5, f32[8,2,256,256]{3,2,1,0:T(8,128)} %get-tuple-element.34.right, f32[2,256,256]{2,1,0:T(8,128)} %get-tuple-element.46.back), custom_call_target="tpu_custom_call" | custom-call | flops 201326592 | bytes 786432 | tf_op jit(solution)/shard_map/rows_back/pallas_call | solution.py:188
  182.0 2.8 %rows_back.7 = f32[2,64,256]{2,1,0:T(8,128)} custom-call(f32[2,2,64,256]{3,2,1,0:T(8,128)} %copy-done.6, f32[8,2,256,256]{3,2,1,0:T(8,128)} %get-tuple-element.34.right, f32[2,256,256]{2,1,0:T(8,128)} %get-tuple-element.46.back), custom_call_target="tpu_custom_call" | custom-call | flops 201326592 | bytes 786432 | tf_op jit(solution)/shard_map/rows_back/pallas_call | solution.py:188
  186.1 3.4 %last.1 = f32[2,256,256]{2,1,0:T(8,128)} custom-call(f32[8,2,256,256]{3,2,1,0:T(8,128)} %get-tuple-element.36.left, f32[2,256,256]{2,1,0:T(8,128)} %get-tuple-element.50.result, f32[2,2,64,256]{3,2,1,0:T(8,128)} %copy-done.3, f32[2,2,64,256]{3,2,1,0:T(8,128)} %copy-done.4, f32[2,2,64,256]{3,2,1,0:T(8,128)} %copy-done.5, f32[2,2,64,256]{3,2,1,0:T(8,128)} %copy-done.6), custom_call_target="tpu_custom_call" | custom-call | flops 805306368 | bytes 1572864 | tf_op jit(solution)/shard_map/last/pallas_call | solution.py:218
  189.6 3.2 %collective-permute-done.22 = f32[2,64,256]{2,1,0:T(8,128)S(1)} collective-permute-done((f32[2,64,256]{2,1,0:T(8,128)}, f32[2,64,256]{2,1,0:T(8,128)S(1)}, u32[]{:S(2)}, u32[]{:S(2)}) %collective-permute-start.22) | collective-permute-done | bytes 131104 | tf_op jit(solution)/shard_map/ppermute | solution.py:22
  (76 shorter events, 16.4 us)
Async XLA Ops:
  0.0 8.3 %collective-permute-start.5 = (f32[1,256,256]{2,1,0:T(8,128)}, f32[1,256,256]{2,1,0:T(8,128)S(1)}, u32[]{:S(2)}, u32[]{:S(2)}) collective-permute-start(f32[1,256,256]{2,1,0:T(8,128)} %bitcast.7), channel_id=1, source_target_pairs={{0,2},{1,3},{2,0},{3,1},{4,6},{5,7},{6,4},{7,5},{8,10},{9,11},{10,... | collective-permute-start | bytes 786440 | tf_op jit(solution)/shard_map/ppermute | solution.py:18
  1.5 13.7 %collective-permute-start = (f32[1,256,256]{2,1,0:T(8,128)}, f32[1,256,256]{2,1,0:T(8,128)S(1)}, u32[]{:S(2)}, u32[]{:S(2)}) collective-permute-start(f32[1,256,256]{2,1,0:T(8,128)} %bitcast.8), channel_id=1, source_target_pairs={{0,8},{1,9},{2,10},{3,11},{4,12},{5,13},{6,14},{7,15},{8,0},{9,1},... | collective-permute-start | bytes 786440 | tf_op jit(solution)/shard_map/ppermute | solution.py:18
  8.3 24.6 %copy-start.7 = (f32[1,256,256]{2,1,0:T(8,128)}, f32[1,256,256]{2,1,0:T(8,128)S(1)}, u32[]{:S(2)}) copy-start(f32[1,256,256]{2,1,0:T(8,128)S(1)} %collective-permute-done.5.first) | copy-start | bytes 786436
  9.3 16.0 %collective-permute-start.6 = (f32[2,256,256]{2,1,0:T(8,128)S(1)}, f32[2,256,256]{2,1,0:T(8,128)S(1)}, u32[]{:S(2)}, u32[]{:S(2)}) collective-permute-start(f32[2,256,256]{2,1,0:T(8,128)S(1)} %pad_maximum_fusion), channel_id=1, source_target_pairs={{0,4},{1,5},{2,6},{3,7},{4,0},{5,1},{6,2},{7,3},{8,12},{9,13},{10,... | collective-permute-start | bytes 1572872 | tf_op jit(solution)/shard_map/ppermute | solution.py:18
  15.2 8.2 %collective-permute-start.1 = (f32[1,256,256]{2,1,0:T(8,128)S(1)}, f32[1,256,256]{2,1,0:T(8,128)S(1)}, u32[]{:S(2)}, u32[]{:S(2)}) collective-permute-start(f32[1,256,256]{2,1,0:T(8,128)S(1)} %collective-permute-done), channel_id=1, source_target_pairs={{0,2},{1,3},{2,0},{3,1},{4,6},{5,7},{6,4},{7,5},{8,10},{9,11},{10,... | collective-permute-start | bytes 786440 | tf_op jit(solution)/shard_map/ppermute | solution.py:18
  23.5 14.5 %copy-start = (f32[2,256,256]{2,1,0:T(8,128)}, f32[2,256,256]{2,1,0:T(8,128)S(1)}, u32[]{:S(2)}) copy-start(f32[2,256,256]{2,1,0:T(8,128)S(1)} %constant_dynamic-update-slice_fusion.first) | copy-start | bytes 1572868
  23.5 14.5 %collective-permute-start.2 = (f32[2,256,256]{2,1,0:T(8,128)S(1)}, f32[2,256,256]{2,1,0:T(8,128)S(1)}, u32[]{:S(2)}, u32[]{:S(2)}) collective-permute-start(f32[2,256,256]{2,1,0:T(8,128)S(1)} %constant_dynamic-update-slice_fusion.first), channel_id=1, source_target_pairs={{0,4},{1,5},{2,6},{3,7},{4,0},{5,1},{6,2},{7,3},{8,12},{9,13},{10,... | collective-permute-start | bytes 1572872 | tf_op jit(solution)/shard_map/ppermute | solution.py:18
  25.3 12.7 %copy-start.9 = (f32[2,256,256]{2,1,0:T(8,128)}, f32[2,256,256]{2,1,0:T(8,128)S(1)}, u32[]{:S(2)}) copy-start(f32[2,256,256]{2,1,0:T(8,128)S(1)} %collective-permute-done.6.first) | copy-start | bytes 1572868
  25.3 12.9 %collective-permute-start.7 = (f32[2,256,256]{2,1,0:T(8,128)S(1)}, f32[2,256,256]{2,1,0:T(8,128)S(1)}, u32[]{:S(2)}, u32[]{:S(2)}) collective-permute-start(f32[2,256,256]{2,1,0:T(8,128)S(1)} %collective-permute-done.6.first), channel_id=1, source_target_pairs={{0,1},{1,0},{2,3},{3,2},{4,5},{5,4},{6,7},{7,6},{8,9},{9,8},{10,11... | collective-permute-start | bytes 1572872 | tf_op jit(solution)/shard_map/ppermute | solution.py:18
  25.3 2.3 %collective-permute-start.9 = (f32[1,256,256]{2,1,0:T(8,128)}, f32[1,256,256]{2,1,0:T(8,128)S(1)}, u32[]{:S(2)}, u32[]{:S(2)}) collective-permute-start(f32[1,256,256]{2,1,0:T(8,128)} %bitcast.10), channel_id=1, source_target_pairs={{0,1},{1,0},{2,3},{3,2},{4,5},{5,4},{6,7},{7,6},{8,9},{9,8},{10,11... | collective-permute-start | bytes 786440 | tf_op jit(solution)/shard_map/ppermute | solution.py:18
  25.8 7.0 %collective-permute-start.8 = (f32[1,256,256]{2,1,0:T(8,128)S(1)}, f32[1,256,256]{2,1,0:T(8,128)S(1)}, u32[]{:S(2)}, u32[]{:S(2)}) collective-permute-start(f32[1,256,256]{2,1,0:T(8,128)S(1)} %collective-permute-done.5.first), channel_id=1, source_target_pairs={{0,1},{1,0},{2,3},{3,2},{4,5},{5,4},{6,7},{7,6},{8,9},{9,8},{10,11... | collective-permute-start | bytes 786440 | tf_op jit(solution)/shard_map/ppermute | solution.py:18
  25.8 25.9 %collective-permute-start.4 = (f32[2,256,256]{2,1,0:T(8,128)S(1)}, f32[2,256,256]{2,1,0:T(8,128)S(1)}, u32[]{:S(2)}, u32[]{:S(2)}) collective-permute-start(f32[2,256,256]{2,1,0:T(8,128)S(1)} %constant_dynamic-update-slice_fusion.first), channel_id=1, source_target_pairs={{0,1},{1,0},{2,3},{3,2},{4,5},{5,4},{6,7},{7,6},{8,9},{9,8},{10,11... | collective-permute-start | bytes 1572872 | tf_op jit(solution)/shard_map/ppermute | solution.py:18
  38.0 7.2 %copy-start.8 = (f32[2,256,256]{2,1,0:T(8,128)}, f32[2,256,256]{2,1,0:T(8,128)S(1)}, u32[]{:S(2)}) copy-start(f32[2,256,256]{2,1,0:T(8,128)S(1)} %collective-permute-done.2.first) | copy-start | bytes 1572868
  38.0 27.2 %collective-permute-start.3 = (f32[2,256,256]{2,1,0:T(8,128)S(1)}, f32[2,256,256]{2,1,0:T(8,128)}, u32[]{:S(2)}, u32[]{:S(2)}) collective-permute-start(f32[2,256,256]{2,1,0:T(8,128)S(1)} %collective-permute-done.2.first), channel_id=1, source_target_pairs={{0,1},{1,0},{2,3},{3,2},{4,5},{5,4},{6,7},{7,6},{8,9},{9,8},{10,11... | collective-permute-start | bytes 1572872 | tf_op jit(solution)/shard_map/ppermute | solution.py:18
  45.2 109.2 %collective-permute-start.13 = (f32[2,2,256,256]{3,2,1,0:T(8,128)}, f32[2,2,256,256]{3,2,1,0:T(8,128)S(1)}, u32[]{:S(2)}, u32[]{:S(2)}) collective-permute-start(f32[2,2,256,256]{3,2,1,0:T(8,128)} %get-tuple-element.37), channel_id=1, source_target_pairs={{0,8},{2,10},{4,12},{6,14},{9,1},{11,3},{13,5},{15,7},{16,24},{18,... | collective-permute-start | bytes 3145736 | tf_op jit(solution)/shard_map/ppermute | solution.py:22
  52.5 12.6 %copy-start.16 = (s32[1,16]{1,0:T(1,128)S(1)}, s32[1,16]{1,0:T(1,128)}, u32[]{:S(2)}) copy-start(s32[1,16]{1,0:T(1,128)} %param.12) | copy-start | bytes 196
  52.5 12.6 %copy-start.17 = (s32[1,16]{1,0:T(1,128)S(1)}, s32[1,16]{1,0:T(1,128)}, u32[]{:S(2)}) copy-start(s32[1,16]{1,0:T(1,128)} %param.11) | copy-start | bytes 196
  52.5 12.6 %copy-start.18 = (s32[1,16]{1,0:T(1,128)S(1)}, s32[1,16]{1,0:T(1,128)}, u32[]{:S(2)}) copy-start(s32[1,16]{1,0:T(1,128)} %param.10) | copy-start | bytes 196
  58.8 102.1 %collective-permute-start.12 = (f32[2,2,256,256]{3,2,1,0:T(8,128)}, f32[2,2,256,256]{3,2,1,0:T(8,128)S(1)}, u32[]{:S(2)}, u32[]{:S(2)}) collective-permute-start(f32[2,2,256,256]{3,2,1,0:T(8,128)} %get-tuple-element.35), channel_id=1, source_target_pairs={{0,8},{2,10},{4,12},{6,14},{9,1},{11,3},{13,5},{15,7},{16,24},{18,... | collective-permute-start | bytes 3145736 | tf_op jit(solution)/shard_map/ppermute | solution.py:22
  60.2 84.9 %collective-permute-start.15 = (f32[1,2,256,256]{3,2,1,0:T(8,128)}, f32[1,2,256,256]{3,2,1,0:T(8,128)}, u32[]{:S(2)}, u32[]{:S(2)}) collective-permute-start(f32[1,2,256,256]{3,2,1,0:T(8,128)} %get-tuple-element.39), channel_id=1, source_target_pairs={{0,8},{2,10},{4,12},{6,14},{9,1},{11,3},{13,5},{15,7},{16,24},{18,... | collective-permute-start | bytes 1572872 | tf_op jit(solution)/shard_map/ppermute | solution.py:22
  63.0 86.5 %collective-permute-start.14 = (f32[1,2,256,256]{3,2,1,0:T(8,128)}, f32[1,2,256,256]{3,2,1,0:T(8,128)}, u32[]{:S(2)}, u32[]{:S(2)}) collective-permute-start(f32[1,2,256,256]{3,2,1,0:T(8,128)} %get-tuple-element.38), channel_id=1, source_target_pairs={{0,8},{2,10},{4,12},{6,14},{9,1},{11,3},{13,5},{15,7},{16,24},{18,... | collective-permute-start | bytes 1572872 | tf_op jit(solution)/shard_map/ppermute | solution.py:22
  65.2 6.3 %copy-start.14 = (s32[4,16]{1,0:T(4,128)}, s32[4,16]{1,0:T(4,128)S(1)}, u32[]{:S(2)}) copy-start(s32[4,16]{1,0:T(4,128)S(1)} %add_add_fusion.own_list) | copy-start | bytes 772
  65.2 68.2 %collective-permute-start.11 = (s32[4,16]{1,0:T(4,128)S(1)}, s32[4,16]{1,0:T(4,128)S(1)}, u32[]{:S(2)}, u32[]{:S(2)}) collective-permute-start(s32[4,16]{1,0:T(4,128)S(1)} %add_add_fusion.own_list), channel_id=1, source_target_pairs={{0,8},{1,9},{2,10},{3,11},{4,12},{5,13},{6,14},{7,15},{8,0},{9,1},... | collective-permute-start | bytes 776 | tf_op jit(solution)/shard_map/ppermute | solution.py:18
  133.4 5.3 %copy-start.15 = (s32[4,16]{1,0:T(4,128)}, s32[4,16]{1,0:T(4,128)S(1)}, u32[]{:S(2)}) copy-start(s32[4,16]{1,0:T(4,128)S(1)} %collective-permute-done.11.other_list) | copy-start | bytes 772
  133.4 33.6 %collective-permute-start.10 = (f32[2,2,64,256]{3,2,1,0:T(8,128)}, f32[2,2,64,256]{3,2,1,0:T(8,128)S(1)}, u32[]{:S(2)}, u32[]{:S(2)}) collective-permute-start(f32[2,2,64,256]{3,2,1,0:T(8,128)} %get-tuple-element.32), channel_id=1, source_target_pairs={{0,8},{2,10},{4,12},{6,14},{9,1},{11,3},{13,5},{15,7},{16,24},{18,... | collective-permute-start | bytes 786440 | tf_op jit(solution)/shard_map/ppermute | solution.py:22
  145.1 26.7 %collective-permute-start.17 = (f32[2,2,64,256]{3,2,1,0:T(8,128)}, f32[2,2,64,256]{3,2,1,0:T(8,128)S(1)}, u32[]{:S(2)}, u32[]{:S(2)}) collective-permute-start(f32[2,2,64,256]{3,2,1,0:T(8,128)} %get-tuple-element.47), channel_id=1, source_target_pairs={{0,8},{2,10},{4,12},{6,14},{9,1},{11,3},{13,5},{15,7},{16,24},{18,... | collective-permute-start | bytes 786440 | tf_op jit(solution)/shard_map/ppermute | solution.py:22
  149.6 27.0 %collective-permute-start.19 = (f32[2,2,64,256]{3,2,1,0:T(8,128)}, f32[2,2,64,256]{3,2,1,0:T(8,128)S(1)}, u32[]{:S(2)}, u32[]{:S(2)}) collective-permute-start(f32[2,2,64,256]{3,2,1,0:T(8,128)} %get-tuple-element.48), channel_id=1, source_target_pairs={{0,8},{2,10},{4,12},{6,14},{9,1},{11,3},{13,5},{15,7},{16,24},{18,... | collective-permute-start | bytes 786440 | tf_op jit(solution)/shard_map/ppermute | solution.py:22
  154.4 26.9 %collective-permute-start.21 = (f32[2,2,64,256]{3,2,1,0:T(8,128)S(1)}, f32[2,2,64,256]{3,2,1,0:T(8,128)S(1)}, u32[]{:S(2)}, u32[]{:S(2)}) collective-permute-start(f32[2,2,64,256]{3,2,1,0:T(8,128)S(1)} %copy-done.19), channel_id=1, source_target_pairs={{0,8},{2,10},{4,12},{6,14},{9,1},{11,3},{13,5},{15,7},{16,24},{18,... | collective-permute-start | bytes 786440 | tf_op jit(solution)/shard_map/ppermute | solution.py:22
  170.5 19.1 %collective-permute-start.16 = (f32[2,64,256]{2,1,0:T(8,128)}, f32[2,64,256]{2,1,0:T(8,128)S(1)}, u32[]{:S(2)}, u32[]{:S(2)}) collective-permute-start(f32[2,64,256]{2,1,0:T(8,128)} %rows_back.4), channel_id=1, source_target_pairs={{8,0},{10,2},{12,4},{14,6},{1,9},{3,11},{5,13},{7,15},{24,16},{26,... | collective-permute-start | bytes 393224 | tf_op jit(solution)/shard_map/ppermute | solution.py:22
  175.2 14.3 %collective-permute-start.18 = (f32[2,64,256]{2,1,0:T(8,128)}, f32[2,64,256]{2,1,0:T(8,128)S(1)}, u32[]{:S(2)}, u32[]{:S(2)}) collective-permute-start(f32[2,64,256]{2,1,0:T(8,128)} %rows_back.5), channel_id=1, source_target_pairs={{8,0},{10,2},{12,4},{14,6},{1,9},{3,11},{5,13},{7,15},{24,16},{26,... | collective-permute-start | bytes 393224 | tf_op jit(solution)/shard_map/ppermute | solution.py:22
  180.0 9.5 %collective-permute-start.20 = (f32[2,64,256]{2,1,0:T(8,128)}, f32[2,64,256]{2,1,0:T(8,128)S(1)}, u32[]{:S(2)}, u32[]{:S(2)}) collective-permute-start(f32[2,64,256]{2,1,0:T(8,128)} %rows_back.6), channel_id=1, source_target_pairs={{8,0},{10,2},{12,4},{14,6},{1,9},{3,11},{5,13},{7,15},{24,16},{26,... | collective-permute-start | bytes 393224 | tf_op jit(solution)/shard_map/ppermute | solution.py:22
  184.8 8.0 %collective-permute-start.22 = (f32[2,64,256]{2,1,0:T(8,128)}, f32[2,64,256]{2,1,0:T(8,128)S(1)}, u32[]{:S(2)}, u32[]{:S(2)}) collective-permute-start(f32[2,64,256]{2,1,0:T(8,128)} %rows_back.7), channel_id=1, source_target_pairs={{8,0},{10,2},{12,4},{14,6},{1,9},{3,11},{5,13},{7,15},{24,16},{26,... | collective-permute-start | bytes 393224 | tf_op jit(solution)/shard_map/ppermute | solution.py:22
  (11 other events, 11.8 us)
where the time goes:
time: 195 us; the launch traced here: 194 us
  waiting for transfers between devices  84.9 us (44%)
  Pallas kernels  65.4 us (34%)
  starting transfers between devices  32.9 us (17%)
  local copies, waits for them, and re-layouts  6.91 us (4%)
  other arithmetic  2.61 us (1%)
    ppermute x11, waiting for transfers between devices, swapped(): return lax.ppermute(value, axis, pairs)  81.6 us
    pallas_call x5, Pallas kernels, blocks_of(): pl.pallas_call(partial(block_kernel, spans), out_shape=shapes, grid_spec=...  27.7 us
    ppermute x12, starting transfers between devices, sent(): lax.ppermute(value, axis, [(source, source ^ mask) for source in senders])  26.5 us
    pallas_call x4, Pallas kernels, finished(): pl.pallas_call(finish_kernel, out_shape=(shape, shape), grid=(size,), in_...  16.8 us
    pallas_call x4, Pallas kernels, rows_back(): pl.pallas_call(partial(back_kernel, low, rows), out_shape=jax.ShapeDtypeS...  11.1 us
    unnamed x41, local copies, waits for them, and re-layouts  6.82 us
    ppermute x11, starting transfers between devices, swapped(): return lax.ppermute(value, axis, pairs)  6.45 us
    pallas_call x1, Pallas kernels, mixed(): pl.pallas_call(mix_kernel, out_shape=(shape, shape), in_specs=[smem, smem...  6.34 us
  transfers between devices with their start and end apart: 23, of which 7 were waited for; matrix products, arithmetic and copies ran while one was open for 1% of the time, Pallas kernels for 34%

commit v1 on v0

--- a/solution.py
+++ b/solution.py
@@ -7,19 +7,20 @@
 from jax.experimental.pallas import tpu as pltpu
 from jax.sharding import PartitionSpec as P
 
+
 F32 = jnp.float32
+VMEM = 24 << 20
 NN = (((1,), (0,)), ((), ()))
 NT = (((1,), (1,)), ((), ()))
 ROWS = (64, 64, 64, 64)
 
 
-def swapped(value, axis, mask):
-    pairs = [(source, source ^ mask) for source in range(lax.axis_size(axis))]
-    return lax.ppermute(value, axis, pairs)
-
-
 def sent(value, axis, mask, senders):
     return lax.ppermute(value, axis, [(source, source ^ mask) for source in senders])
+
+
+def swapped(value, axis, mask):
+    return sent(value, axis, mask, range(lax.axis_size(axis)))
 
 
 def halves(value):
@@ -91,6 +92,7 @@
         cost_estimate=pl.CostEstimate(
             flops=size * 72 * width**3, bytes_accessed=size * 28 * width**2, transcendentals=0
         ),
+        compiler_params=pltpu.CompilerParams(vmem_limit_bytes=VMEM),
         name="blocks",
     )(place, *operands)
     return outs[:-1], outs[-1]
@@ -126,6 +128,7 @@
         cost_estimate=pl.CostEstimate(
             flops=blocks.size * 4, bytes_accessed=blocks.size * 12, transcendentals=0
         ),
+        compiler_params=pltpu.CompilerParams(vmem_limit_bytes=VMEM),
         name="mix",
     )(own_list, other_list, place, blocks)
 
@@ -170,6 +173,7 @@
         cost_estimate=pl.CostEstimate(
             flops=size * 48 * width**3, bytes_accessed=size * 24 * width**2, transcendentals=0
         ),
+        compiler_params=pltpu.CompilerParams(vmem_limit_bytes=VMEM),
         name="finish",
     )(chunk, left, right, *sums)
 
@@ -198,11 +202,12 @@
         cost_estimate=pl.CostEstimate(
             flops=size * 24 * rows * width**2, bytes_accessed=12 * width**2, transcendentals=0
         ),
+        compiler_params=pltpu.CompilerParams(vmem_limit_bytes=VMEM),
         name="rows_back",
     )(chunk, right, back)
 
 
-def last_kernel(spans, left, result, *refs):
+def last_kernel(left, result, *refs):
     chunks, out = refs[:-1], refs[-1]
     real, imag = result[0], result[1]
     for k in range(left.shape[0]):
@@ -213,10 +218,10 @@
     out[0], out[1] = real, imag
 
 
-def last_added(chunks, left, start, result, spans):
+def last_added(chunks, left, start, result):
     size, width = chunks[0].shape[0], chunks[0].shape[-1]
     return pl.pallas_call(
-        partial(last_kernel, spans),
+        last_kernel,
         out_shape=jax.ShapeDtypeStruct(result.shape, F32),
         grid=(1,),
         in_specs=[
@@ -228,6 +233,7 @@
         cost_estimate=pl.CostEstimate(
             flops=size * 24 * width**3, bytes_accessed=24 * width**2, transcendentals=0
         ),
+        compiler_params=pltpu.CompilerParams(vmem_limit_bytes=VMEM),
         name="last",
     )(left, result, *chunks)
 
@@ -259,37 +265,37 @@
     own_list = jnp.concatenate([pair_left, pair_right, pair_weight, count])
 
     w0 = meson_src[None]
+    w4 = swapped(w0, axis, half)
     s0 = whole(w0)
-    w4 = swapped(w0, axis, half)
     w1 = swapped(w0, axis, group)
+    other_list = swapped(own_list, axis, half)
     s1 = whole(w1)
     w23 = swapped(jnp.concatenate([w0, w1]), axis, 2 * group)
     s23 = whole(w23)
     w45 = jnp.concatenate([w4, swapped(w4, axis, group)])
     s45 = whole(w45)
     s67 = whole(swapped(w45, axis, 2 * group))
-    other_list = swapped(own_list, axis, half)
 
     lows = [sum(ROWS[:r]) * width // 256 for r in range(len(ROWS))]
     spans = [(low, rows * width // 256) for low, rows in zip(lows, ROWS, strict=True)]
     blocks, arrived, start = None, [], 0
-    for source in (s0, s1, s23, s45):
+    for name, source in zip(("0", "1", "23", "45"), (s0, s1, s23, s45), strict=True):
         (chunk,), blocks = blocks_of(place, meson, peram, *source, blocks, start, [(0, width)])
-        arrived.append((start, sent(chunk, axis, half, senders)))
+        arrived.append((name, start, sent(chunk, axis, half, senders)))
         start += source[0].shape[0]
     chunks, blocks = blocks_of(place, meson, peram, *s67, blocks, start, spans)
     chunks = [sent(chunk, axis, half, senders) for chunk in chunks]
 
     left, right = mixed(own_list, other_list, place, blocks)
     sums = ()
-    for at, chunk in arrived:
+    for name, at, chunk in arrived:
         sums = finished(chunk, left, right, at, sums)
     result, back = sums
-    returned = [
-        sent(rows_back(chunk, right, start, back, low), axis, half, receivers)
-        for chunk, (low, _) in zip(chunks, spans, strict=True)
-    ]
-    result = last_added(chunks, left, start, result, spans)
+    returned = []
+    for chunk, (low, _) in zip(chunks, spans, strict=True):
+        rows = rows_back(chunk, right, start, back, low)
+        returned.append(sent(rows, axis, half, receivers))
+    result = last_added(chunks, left, start, result)
     return jnp.where(is_sender, jnp.concatenate(returned, axis=1), result)[None]
 
 

time: 195 us -> 166 us (0.85)
  Pallas kernels: 65.4 us -> 28.2 us
  waiting for transfers between devices: 84.9 us -> 96.3 us
    ppermute x12 -> x23, waiting for transfers between devices: 3.24 us -> 96.3 us  [sent(): lax.ppermute(value, axis, [(source, source ^ mask) for source in senders])]
    ppermute x11 -> x0, waiting for transfers between devices: 81.6 us -> none  [swapped(): return lax.ppermute(value, axis, pairs)]
    pallas_call x5, Pallas kernels: 27.7 us -> 15.1 us  [blocks_of(): pl.pallas_call(partial(block_kernel, spans), out_shape=shapes, grid_spec=...]
    pallas_call x4, Pallas kernels: 16.8 us -> 6.68 us  [finished(): pl.pallas_call(finish_kernel, out_shape=(shape, shape), grid=(size,), in_...]
    pallas_call x4, Pallas kernels: 11.1 us -> 2.74 us  [rows_back(): pl.pallas_call(partial(back_kernel, low, rows), out_shape=jax.ShapeDtypeS...]
    ppermute x11 -> x0, starting transfers between devices: 6.45 us -> none  [swapped(): return lax.ppermute(value, axis, pairs)]
    ppermute x12 -> x23, starting transfers between devices: 26.5 us -> 31.1 us  [sent(): lax.ppermute(value, axis, [(source, source ^ mask) for source in senders])]
    pallas_call x1, Pallas kernels: 6.34 us -> 2.69 us  [mixed(): pl.pallas_call(mix_kernel, out_shape=(shape, shape), in_specs=[smem, smem...]
  transfers between devices with their start and end apart: 23 -> 23, of which waited for: 7 -> 9; matrix products, arithmetic and copies ran while one was open for 1% -> 1% of each run, Pallas kernels for 34% -> 17%
where the time goes in v1:
time: 166 us; the launch traced here: 165 us
  waiting for transfers between devices  96.3 us (58%)
  starting transfers between devices  31.1 us (19%)
  Pallas kernels  28.2 us (17%)
  local copies, waits for them, and re-layouts  6.49 us (4%)
  other arithmetic  1.99 us (1%)
    ppermute x23, waiting for transfers between devices, sent(): lax.ppermute(value, axis, [(source, source ^ mask) for source in senders])  96.3 us
    ppermute x23, starting transfers between devices, sent(): lax.ppermute(value, axis, [(source, source ^ mask) for source in senders])  31.1 us
    pallas_call x5, Pallas kernels, blocks_of(): pl.pallas_call(partial(block_kernel, spans), out_shape=shapes, grid_spec=...  15.1 us
    pallas_call x4, Pallas kernels, finished(): pl.pallas_call(finish_kernel, out_shape=(shape, shape), grid=(size,), in_...  6.68 us
    unnamed x17, local copies, waits for them, and re-layouts  6.4 us
  transfers between devices with their start and end apart: 23, of which 9 were waited for; matrix products, arithmetic and copies ran while one was open for 1% of the time, Pallas kernels for 17%

profile of v1, /device:TPU:8, one launch (start us, length us, event | category | flops | bytes accessed | tf_op | source)
XLA Modules:
  0.0 165.1 jit_solution(4282662517652553781)
XLA Ops:
  0.0 1.5 collective-permute-start.5
  1.5 2.6 %collective-permute-start = (f32[1,256,256]{2,1,0:T(8,128)}, f32[1,256,256]{2,1,0:T(8,128)S(1)}, u32[]{:S(2)}, u32[]{:S(2)}) collective-permute-start(f32[1,256,256]{2,1,0:T(8,128)} %bitcast.8), channel_id=1, source_target_pairs={{0,8},{1,9},{2,10},{3,11},{4,12},{5,13},{6,14},{7,15},{8,0},{9,1},... | collective-permute-start | bytes 786440 | tf_op jit(solution)/shard_map/ppermute | solution.py:19
  4.1 4.2 %collective-permute-done.5.first = f32[1,256,256]{2,1,0:T(8,128)S(1)} collective-permute-done((f32[1,256,256]{2,1,0:T(8,128)}, f32[1,256,256]{2,1,0:T(8,128)S(1)}, u32[]{:S(2)}, u32[]{:S(2)}) %collective-permute-start.5) | collective-permute-done | bytes 262176 | tf_op jit(solution)/shard_map/ppermute | solution.py:19
  9.5 5.7 %collective-permute-done = f32[1,256,256]{2,1,0:T(8,128)S(1)} collective-permute-done((f32[1,256,256]{2,1,0:T(8,128)}, f32[1,256,256]{2,1,0:T(8,128)S(1)}, u32[]{:S(2)}, u32[]{:S(2)}) %collective-permute-start) | collective-permute-done | bytes 262176 | tf_op jit(solution)/shard_map/ppermute | solution.py:19
  15.8 7.7 %collective-permute-done.1 = f32[1,256,256]{2,1,0:T(8,128)S(1)} collective-permute-done((f32[1,256,256]{2,1,0:T(8,128)S(1)}, f32[1,256,256]{2,1,0:T(8,128)S(1)}, u32[]{:S(2)}, u32[]{:S(2)}) %collective-permute-start.1) | collective-permute-done | bytes 262176 | tf_op jit(solution)/shard_map/ppermute | solution.py:19
  23.8 1.5 collective-permute-done.6.first
  26.4 1.2 collective-permute-done.9.second
  27.6 2.2 %copy-done = f32[1,8,2,256,256]{4,3,2,1,0:T(8,128)S(1)} copy-done((f32[1,8,2,256,256]{4,3,2,1,0:T(8,128)S(1)}, f32[1,8,2,256,256]{4,3,2,1,0:T(8,128)}, u32[]{:S(2)}) %copy-start) | copy-done | bytes 4194328
  31.8 2.1 %blocks.5 = (f32[1,2,256,256]{3,2,1,0:T(8,128)S(1)}, f32[8,2,256,256]{3,2,1,0:T(8,128)S(1)}) custom-call(s32[3]{0:T(128)S(1)} %pad_add_fusion.place, f32[1,2,256,256]{3,2,1,0:T(8,128)S(1)} %copy-done.3, f32[1,8,2,256,256]{4,3,2,1,0:T(8,128)S(1)} %copy-done, f32[1,256,256]{2,1,0:T(8,128)S(1)} %bitcast.11, f32[1,256,256]{2,1,0:T(8,128)S(1)} %collective-permute-done.9.second), custom_call_target="tpu_custom_call" | custom-call | flops 1207959552 | bytes 1835008 | tf_op jit(solution)/shard_map/blocks/pallas_call | solution.py:85
  33.9 2.1 %blocks.6 = (f32[1,2,256,256]{3,2,1,0:T(8,128)S(1)}, f32[8,2,256,256]{3,2,1,0:T(8,128)S(1)}) custom-call(s32[3]{0:T(128)S(1)} %pad_add_fusion.place, f32[1,2,256,256]{3,2,1,0:T(8,128)S(1)} %copy-done.3, f32[1,8,2,256,256]{4,3,2,1,0:T(8,128)S(1)} %copy-done, f32[1,256,256]{2,1,0:T(8,128)S(1)} %collective-permute-done.5.first, ...), custom_call_target="tpu_custom_call", output_to_operand_aliasing={{1}: (5, {})} | custom-call | flops 1207959552 | bytes 1835008 | tf_op jit(solution)/shard_map/blocks/pallas_call | solution.py:85
  36.5 3.6 %blocks.7 = (f32[2,2,256,256]{3,2,1,0:T(8,128)S(1)}, f32[8,2,256,256]{3,2,1,0:T(8,128)S(1)}) custom-call(s32[3]{0:T(128)S(1)} %pad_add_fusion.place, f32[1,2,256,256]{3,2,1,0:T(8,128)S(1)} %copy-done.3, f32[1,8,2,256,256]{4,3,2,1,0:T(8,128)S(1)} %copy-done, f32[2,256,256]{2,1,0:T(8,128)S(1)} %collective-permute-done.6.first, ...), custom_call_target="tpu_custom_call", output_to_operand_aliasing={{1}: (5, {})} | custom-call | flops 2415919104 | bytes 3670016 | tf_op jit(solution)/shard_map/blocks/pallas_call | solution.py:85
  40.2 6.4 %collective-permute-start.13 = (f32[2,2,256,256]{3,2,1,0:T(8,128)S(1)}, f32[2,2,256,256]{3,2,1,0:T(8,128)S(1)}, u32[]{:S(2)}, u32[]{:S(2)}) collective-permute-start(f32[2,2,256,256]{3,2,1,0:T(8,128)S(1)} %get-tuple-element.37), channel_id=1, source_target_pairs={{0,8},{2,10},{4,12},{6,14},{9,1},{11,3},{13,5},{15,7},{16,24},{18,... | collective-permute-start | bytes 3145736 | tf_op jit(solution)/shard_map/ppermute | solution.py:19
  46.6 3.6 %blocks.8 = (f32[2,2,256,256]{3,2,1,0:T(8,128)S(1)}, f32[8,2,256,256]{3,2,1,0:T(8,128)S(1)}) custom-call(s32[3]{0:T(128)S(1)} %pad_add_fusion.place, f32[1,2,256,256]{3,2,1,0:T(8,128)S(1)} %copy-done.3, f32[1,8,2,256,256]{4,3,2,1,0:T(8,128)S(1)} %copy-done, ...), custom_call_target="tpu_custom_call", output_to_operand_aliasing={{1}: (5, {})} | custom-call | flops 2415919104 | bytes 3670016 | tf_op jit(solution)/shard_map/blocks/pallas_call | solution.py:85
  50.3 1.4 collective-permute-start.12
  51.6 1.3 collective-permute-start.15
  53.7 1.3 collective-permute-start.14
  55.1 3.6 %blocks.9 = (f32[2,2,64,256]{3,2,1,0:T(8,128)S(1)}, f32[2,2,64,256]{3,2,1,0:T(8,128)S(1)}, f32[2,2,64,256]{3,2,1,0:T(8,128)S(1)}, f32[2,2,64,256]{3,2,1,0:T(8,128)S(1)}, f32[8,2,256,256]{3,2,1,0:T(8,128)S(1)}) custom-call(s32[3]{0:T(128)S(1)} %pad_add_fusion.place, f32[1,2,256,256]{3,2,1,0:T(8,128)S(1)} %copy-done.3, ...), custom_call_target="tpu_custom_call", output_to_operand_aliasing={{4}: (5, {})} | custom-call | flops 2415919104 | bytes 3670016 | tf_op jit(solution)/shard_map/blocks/pallas_call | solution.py:85
  58.8 72.1 %collective-permute-done.11.other_list = s32[4,16]{1,0:T(4,128)S(1)} collective-permute-done((s32[4,16]{1,0:T(4,128)S(1)}, s32[4,16]{1,0:T(4,128)S(1)}, u32[]{:S(2)}, u32[]{:S(2)}) %collective-permute-start.11) | collective-permute-done | bytes 288 | tf_op jit(solution)/shard_map/ppermute | solution.py:19
  130.9 5.3 %collective-permute-start.10 = (f32[2,2,64,256]{3,2,1,0:T(8,128)S(1)}, f32[2,2,64,256]{3,2,1,0:T(8,128)S(1)}, u32[]{:S(2)}, u32[]{:S(2)}) collective-permute-start(f32[2,2,64,256]{3,2,1,0:T(8,128)S(1)} %get-tuple-element.32), channel_id=1, source_target_pairs={{0,8},{2,10},{4,12},{6,14},{9,1},{11,3},{13,5},{15,7},{16,24},{18,... | collective-permute-start | bytes 786440 | tf_op jit(solution)/shard_map/ppermute | solution.py:19
  136.2 2.7 %mix.1 = (f32[8,2,256,256]{3,2,1,0:T(8,128)S(1)}, f32[8,2,256,256]{3,2,1,0:T(8,128)S(1)}) custom-call(s32[4,16]{1,0:T(4,128)S(1)} %add_add_fusion.own_list, s32[4,16]{1,0:T(4,128)S(1)} %collective-permute-done.11.other_list, s32[3]{0:T(128)S(1)} %pad_add_fusion.place, f32[8,2,256,256]{3,2,1,0:T(8,128)S(1)} %get-tuple-element.33.blocks), custom_call_target="tpu_custom_call" | custom-call | flops 4194304 | bytes 12582912 | tf_op jit(solution)/shard_map/mix/pallas_call | solution.py:123
  138.9 1.3 collective-permute-start.17
  141.2 1.3 collective-permute-start.19
  143.6 1.5 collective-permute-start.21
  145.1 2.4 %finish.6 = (f32[2,256,256]{2,1,0:T(8,128)S(1)}, f32[2,256,256]{2,1,0:T(8,128)S(1)}) custom-call(f32[2,2,256,256]{3,2,1,0:T(8,128)S(1)} %collective-permute-done.13.chunk, f32[8,2,256,256]{3,2,1,0:T(8,128)S(1)} %get-tuple-element.36.left, f32[8,2,256,256]{3,2,1,0:T(8,128)S(1)} %get-tuple-element.34.right, f32[2,256,256]{2,1,0:T(8,128)S(1)} %get-tuple-element.42.refs_0_, ...), custom_call_target="tpu_custom_call" | custom-call | flops 1610612736 | bytes 3145728 | tf_op jit(solution)/shard_map/finish/pallas_call | solution.py:162
  147.5 2.3 %finish.7 = (f32[2,256,256]{2,1,0:T(8,128)S(1)}, f32[2,256,256]{2,1,0:T(8,128)S(1)}) custom-call(f32[2,2,256,256]{3,2,1,0:T(8,128)S(1)} %collective-permute-done.12.chunk, f32[8,2,256,256]{3,2,1,0:T(8,128)S(1)} %get-tuple-element.36.left, f32[8,2,256,256]{3,2,1,0:T(8,128)S(1)} %get-tuple-element.34.right, f32[2,256,256]{2,1,0:T(8,128)S(1)} %get-tuple-element.44.refs_0_, ...), custom_call_target="tpu_custom_call" | custom-call | flops 1610612736 | bytes 3145728 | tf_op jit(solution)/shard_map/finish/pallas_call | solution.py:162
  150.5 1.3 collective-permute-start.16
  152.5 1.3 collective-permute-start.18
  154.5 1.3 collective-permute-start.20
  156.5 1.3 collective-permute-start.22
  157.8 2.2 %copy-done.2 = f32[8,2,256,256]{3,2,1,0:T(8,128)S(1)} copy-done((f32[8,2,256,256]{3,2,1,0:T(8,128)S(1)}, f32[8,2,256,256]{3,2,1,0:T(8,128)}, u32[]{:S(2)}) %copy-start.2) | copy-done | bytes 4194328
  161.0 1.3 collective-permute-done.20
  162.3 2.0 %collective-permute-done.22 = f32[2,64,256]{2,1,0:T(8,128)S(1)} collective-permute-done((f32[2,64,256]{2,1,0:T(8,128)S(1)}, f32[2,64,256]{2,1,0:T(8,128)S(1)}, u32[]{:S(2)}, u32[]{:S(2)}) %collective-permute-start.22) | collective-permute-done | bytes 131104 | tf_op jit(solution)/shard_map/ppermute | solution.py:19
  (52 shorter events, 12.6 us)
Async XLA Ops:
  0.0 8.3 %collective-permute-start.5 = (f32[1,256,256]{2,1,0:T(8,128)}, f32[1,256,256]{2,1,0:T(8,128)S(1)}, u32[]{:S(2)}, u32[]{:S(2)}) collective-permute-start(f32[1,256,256]{2,1,0:T(8,128)} %bitcast.7), channel_id=1, source_target_pairs={{0,2},{1,3},{2,0},{3,1},{4,6},{5,7},{6,4},{7,5},{8,10},{9,11},{10,... | collective-permute-start | bytes 786440 | tf_op jit(solution)/shard_map/ppermute | solution.py:19
  1.5 13.7 %collective-permute-start = (f32[1,256,256]{2,1,0:T(8,128)}, f32[1,256,256]{2,1,0:T(8,128)S(1)}, u32[]{:S(2)}, u32[]{:S(2)}) collective-permute-start(f32[1,256,256]{2,1,0:T(8,128)} %bitcast.8), channel_id=1, source_target_pairs={{0,8},{1,9},{2,10},{3,11},{4,12},{5,13},{6,14},{7,15},{8,0},{9,1},... | collective-permute-start | bytes 786440 | tf_op jit(solution)/shard_map/ppermute | solution.py:19
  9.2 16.1 %collective-permute-start.6 = (f32[2,256,256]{2,1,0:T(8,128)S(1)}, f32[2,256,256]{2,1,0:T(8,128)S(1)}, u32[]{:S(2)}, u32[]{:S(2)}) collective-permute-start(f32[2,256,256]{2,1,0:T(8,128)S(1)} %pad_maximum_fusion), channel_id=1, source_target_pairs={{0,4},{1,5},{2,6},{3,7},{4,0},{5,1},{6,2},{7,3},{8,12},{9,13},{10,... | collective-permute-start | bytes 1572872 | tf_op jit(solution)/shard_map/ppermute | solution.py:19
  15.2 8.2 %collective-permute-start.1 = (f32[1,256,256]{2,1,0:T(8,128)S(1)}, f32[1,256,256]{2,1,0:T(8,128)S(1)}, u32[]{:S(2)}, u32[]{:S(2)}) collective-permute-start(f32[1,256,256]{2,1,0:T(8,128)S(1)} %collective-permute-done), channel_id=1, source_target_pairs={{0,2},{1,3},{2,0},{3,1},{4,6},{5,7},{6,4},{7,5},{8,10},{9,11},{10,... | collective-permute-start | bytes 786440 | tf_op jit(solution)/shard_map/ppermute | solution.py:19
  23.5 13.1 %collective-permute-start.2 = (f32[2,256,256]{2,1,0:T(8,128)S(1)}, f32[2,256,256]{2,1,0:T(8,128)S(1)}, u32[]{:S(2)}, u32[]{:S(2)}) collective-permute-start(f32[2,256,256]{2,1,0:T(8,128)S(1)} %constant_dynamic-update-slice_fusion.first), channel_id=1, source_target_pairs={{0,4},{1,5},{2,6},{3,7},{4,0},{5,1},{6,2},{7,3},{8,12},{9,13},{10,... | collective-permute-start | bytes 1572872 | tf_op jit(solution)/shard_map/ppermute | solution.py:19
  25.3 11.2 %collective-permute-start.7 = (f32[2,256,256]{2,1,0:T(8,128)S(1)}, f32[2,256,256]{2,1,0:T(8,128)S(1)}, u32[]{:S(2)}, u32[]{:S(2)}) collective-permute-start(f32[2,256,256]{2,1,0:T(8,128)S(1)} %collective-permute-done.6.first), channel_id=1, source_target_pairs={{0,1},{1,0},{2,3},{3,2},{4,5},{5,4},{6,7},{7,6},{8,9},{9,8},{10,11... | collective-permute-start | bytes 1572872 | tf_op jit(solution)/shard_map/ppermute | solution.py:19
  25.3 2.3 %collective-permute-start.9 = (f32[1,256,256]{2,1,0:T(8,128)}, f32[1,256,256]{2,1,0:T(8,128)S(1)}, u32[]{:S(2)}, u32[]{:S(2)}) collective-permute-start(f32[1,256,256]{2,1,0:T(8,128)} %bitcast.10), channel_id=1, source_target_pairs={{0,1},{1,0},{2,3},{3,2},{4,5},{5,4},{6,7},{7,6},{8,9},{9,8},{10,11... | collective-permute-start | bytes 786440 | tf_op jit(solution)/shard_map/ppermute | solution.py:19
  25.8 8.0 %collective-permute-start.8 = (f32[1,256,256]{2,1,0:T(8,128)S(1)}, f32[1,256,256]{2,1,0:T(8,128)S(1)}, u32[]{:S(2)}, u32[]{:S(2)}) collective-permute-start(f32[1,256,256]{2,1,0:T(8,128)S(1)} %collective-permute-done.5.first), channel_id=1, source_target_pairs={{0,1},{1,0},{2,3},{3,2},{4,5},{5,4},{6,7},{7,6},{8,9},{9,8},{10,11... | collective-permute-start | bytes 786440 | tf_op jit(solution)/shard_map/ppermute | solution.py:19
  25.8 20.7 %collective-permute-start.4 = (f32[2,256,256]{2,1,0:T(8,128)S(1)}, f32[2,256,256]{2,1,0:T(8,128)S(1)}, u32[]{:S(2)}, u32[]{:S(2)}) collective-permute-start(f32[2,256,256]{2,1,0:T(8,128)S(1)} %constant_dynamic-update-slice_fusion.first), channel_id=1, source_target_pairs={{0,1},{1,0},{2,3},{3,2},{4,5},{5,4},{6,7},{7,6},{8,9},{9,8},{10,11... | collective-permute-start | bytes 1572872 | tf_op jit(solution)/shard_map/ppermute | solution.py:19
  27.6 2.2 %copy-start = (f32[1,8,2,256,256]{4,3,2,1,0:T(8,128)S(1)}, f32[1,8,2,256,256]{4,3,2,1,0:T(8,128)}, u32[]{:S(2)}) copy-start(f32[1,8,2,256,256]{4,3,2,1,0:T(8,128)} %tau.9) | copy-start | bytes 12582916
  29.8 1.0 copy-start.3
  30.8 0.9 copy-start.4
  36.5 18.6 %collective-permute-start.3 = (f32[2,256,256]{2,1,0:T(8,128)S(1)}, f32[2,256,256]{2,1,0:T(8,128)S(1)}, u32[]{:S(2)}, u32[]{:S(2)}) collective-permute-start(f32[2,256,256]{2,1,0:T(8,128)S(1)} %collective-permute-done.2.first), channel_id=1, source_target_pairs={{0,1},{1,0},{2,3},{3,2},{4,5},{5,4},{6,7},{7,6},{8,9},{9,8},{10,11... | collective-permute-start | bytes 1572872 | tf_op jit(solution)/shard_map/ppermute | solution.py:19
  40.2 103.4 %collective-permute-start.13 = (f32[2,2,256,256]{3,2,1,0:T(8,128)S(1)}, f32[2,2,256,256]{3,2,1,0:T(8,128)S(1)}, u32[]{:S(2)}, u32[]{:S(2)}) collective-permute-start(f32[2,2,256,256]{3,2,1,0:T(8,128)S(1)} %get-tuple-element.37), channel_id=1, source_target_pairs={{0,8},{2,10},{4,12},{6,14},{9,1},{11,3},{13,5},{15,7},{16,24},{18,... | collective-permute-start | bytes 3145736 | tf_op jit(solution)/shard_map/ppermute | solution.py:19
  46.6 8.4 %copy-start.5 = (s32[1,16]{1,0:T(1,128)S(1)}, s32[1,16]{1,0:T(1,128)}, u32[]{:S(2)}) copy-start(s32[1,16]{1,0:T(1,128)} %param.12) | copy-start | bytes 196
  46.6 8.4 %copy-start.6 = (s32[1,16]{1,0:T(1,128)S(1)}, s32[1,16]{1,0:T(1,128)}, u32[]{:S(2)}) copy-start(s32[1,16]{1,0:T(1,128)} %param.11) | copy-start | bytes 196
  46.6 8.4 %copy-start.7 = (s32[1,16]{1,0:T(1,128)S(1)}, s32[1,16]{1,0:T(1,128)}, u32[]{:S(2)}) copy-start(s32[1,16]{1,0:T(1,128)} %param.10) | copy-start | bytes 196
  50.3 97.2 %collective-permute-start.12 = (f32[2,2,256,256]{3,2,1,0:T(8,128)S(1)}, f32[2,2,256,256]{3,2,1,0:T(8,128)S(1)}, u32[]{:S(2)}, u32[]{:S(2)}) collective-permute-start(f32[2,2,256,256]{3,2,1,0:T(8,128)S(1)} %get-tuple-element.35), channel_id=1, source_target_pairs={{0,8},{2,10},{4,12},{6,14},{9,1},{11,3},{13,5},{15,7},{16,24},{18,... | collective-permute-start | bytes 3145736 | tf_op jit(solution)/shard_map/ppermute | solution.py:19
  51.6 87.3 %collective-permute-start.15 = (f32[1,2,256,256]{3,2,1,0:T(8,128)S(1)}, f32[1,2,256,256]{3,2,1,0:T(8,128)S(1)}, u32[]{:S(2)}, u32[]{:S(2)}) collective-permute-start(f32[1,2,256,256]{3,2,1,0:T(8,128)S(1)} %get-tuple-element.39), channel_id=1, source_target_pairs={{0,8},{2,10},{4,12},{6,14},{9,1},{11,3},{13,5},{15,7},{16,24},{18,... | collective-permute-start | bytes 1572872 | tf_op jit(solution)/shard_map/ppermute | solution.py:19
  53.7 87.5 %collective-permute-start.14 = (f32[1,2,256,256]{3,2,1,0:T(8,128)S(1)}, f32[1,2,256,256]{3,2,1,0:T(8,128)S(1)}, u32[]{:S(2)}, u32[]{:S(2)}) collective-permute-start(f32[1,2,256,256]{3,2,1,0:T(8,128)S(1)} %get-tuple-element.38), channel_id=1, source_target_pairs={{0,8},{2,10},{4,12},{6,14},{9,1},{11,3},{13,5},{15,7},{16,24},{18,... | collective-permute-start | bytes 1572872 | tf_op jit(solution)/shard_map/ppermute | solution.py:19
  55.1 75.8 %collective-permute-start.11 = (s32[4,16]{1,0:T(4,128)S(1)}, s32[4,16]{1,0:T(4,128)S(1)}, u32[]{:S(2)}, u32[]{:S(2)}) collective-permute-start(s32[4,16]{1,0:T(4,128)S(1)} %add_add_fusion.own_list), channel_id=1, source_target_pairs={{0,8},{1,9},{2,10},{3,11},{4,12},{5,13},{6,14},{7,15},{8,0},{9,1},... | collective-permute-start | bytes 776 | tf_op jit(solution)/shard_map/ppermute | solution.py:19
  130.9 18.9 %collective-permute-start.10 = (f32[2,2,64,256]{3,2,1,0:T(8,128)S(1)}, f32[2,2,64,256]{3,2,1,0:T(8,128)S(1)}, u32[]{:S(2)}, u32[]{:S(2)}) collective-permute-start(f32[2,2,64,256]{3,2,1,0:T(8,128)S(1)} %get-tuple-element.32), channel_id=1, source_target_pairs={{0,8},{2,10},{4,12},{6,14},{9,1},{11,3},{13,5},{15,7},{16,24},{18,... | collective-permute-start | bytes 786440 | tf_op jit(solution)/shard_map/ppermute | solution.py:19
  138.9 8.6 %copy-start.1 = (f32[8,2,256,256]{3,2,1,0:T(8,128)}, f32[8,2,256,256]{3,2,1,0:T(8,128)S(1)}, u32[]{:S(2)}) copy-start(f32[8,2,256,256]{3,2,1,0:T(8,128)S(1)} %get-tuple-element.36.left) | copy-start | bytes 12582916
  138.9 12.9 %collective-permute-start.17 = (f32[2,2,64,256]{3,2,1,0:T(8,128)S(1)}, f32[2,2,64,256]{3,2,1,0:T(8,128)S(1)}, u32[]{:S(2)}, u32[]{:S(2)}) collective-permute-start(f32[2,2,64,256]{3,2,1,0:T(8,128)S(1)} %get-tuple-element.47), channel_id=1, source_target_pairs={{0,8},{2,10},{4,12},{6,14},{9,1},{11,3},{13,5},{15,7},{16,24},{18,... | collective-permute-start | bytes 786440 | tf_op jit(solution)/shard_map/ppermute | solution.py:19
  141.2 12.6 %collective-permute-start.19 = (f32[2,2,64,256]{3,2,1,0:T(8,128)S(1)}, f32[2,2,64,256]{3,2,1,0:T(8,128)S(1)}, u32[]{:S(2)}, u32[]{:S(2)}) collective-permute-start(f32[2,2,64,256]{3,2,1,0:T(8,128)S(1)} %get-tuple-element.48), channel_id=1, source_target_pairs={{0,8},{2,10},{4,12},{6,14},{9,1},{11,3},{13,5},{15,7},{16,24},{18,... | collective-permute-start | bytes 786440 | tf_op jit(solution)/shard_map/ppermute | solution.py:19
  143.6 12.2 %collective-permute-start.21 = (f32[2,2,64,256]{3,2,1,0:T(8,128)S(1)}, f32[2,2,64,256]{3,2,1,0:T(8,128)S(1)}, u32[]{:S(2)}, u32[]{:S(2)}) collective-permute-start(f32[2,2,64,256]{3,2,1,0:T(8,128)S(1)} %get-tuple-element.49), channel_id=1, source_target_pairs={{0,8},{2,10},{4,12},{6,14},{9,1},{11,3},{13,5},{15,7},{16,24},{18,... | collective-permute-start | bytes 786440 | tf_op jit(solution)/shard_map/ppermute | solution.py:19
  150.5 10.5 %collective-permute-start.16 = (f32[2,64,256]{2,1,0:T(8,128)S(1)}, f32[2,64,256]{2,1,0:T(8,128)S(1)}, u32[]{:S(2)}, u32[]{:S(2)}) collective-permute-start(f32[2,64,256]{2,1,0:T(8,128)S(1)} %rows_back.4), channel_id=1, source_target_pairs={{8,0},{10,2},{12,4},{14,6},{1,9},{3,11},{5,13},{7,15},{24,16},{26,... | collective-permute-start | bytes 393224 | tf_op jit(solution)/shard_map/ppermute | solution.py:19
  152.5 8.5 %collective-permute-start.18 = (f32[2,64,256]{2,1,0:T(8,128)S(1)}, f32[2,64,256]{2,1,0:T(8,128)S(1)}, u32[]{:S(2)}, u32[]{:S(2)}) collective-permute-start(f32[2,64,256]{2,1,0:T(8,128)S(1)} %rows_back.5), channel_id=1, source_target_pairs={{8,0},{10,2},{12,4},{14,6},{1,9},{3,11},{5,13},{7,15},{24,16},{26,... | collective-permute-start | bytes 393224 | tf_op jit(solution)/shard_map/ppermute | solution.py:19
  154.5 7.8 %collective-permute-start.20 = (f32[2,64,256]{2,1,0:T(8,128)S(1)}, f32[2,64,256]{2,1,0:T(8,128)S(1)}, u32[]{:S(2)}, u32[]{:S(2)}) collective-permute-start(f32[2,64,256]{2,1,0:T(8,128)S(1)} %rows_back.6), channel_id=1, source_target_pairs={{8,0},{10,2},{12,4},{14,6},{1,9},{3,11},{5,13},{7,15},{24,16},{26,... | collective-permute-start | bytes 393224 | tf_op jit(solution)/shard_map/ppermute | solution.py:19
  156.5 7.8 %collective-permute-start.22 = (f32[2,64,256]{2,1,0:T(8,128)S(1)}, f32[2,64,256]{2,1,0:T(8,128)S(1)}, u32[]{:S(2)}, u32[]{:S(2)}) collective-permute-start(f32[2,64,256]{2,1,0:T(8,128)S(1)} %rows_back.7), channel_id=1, source_target_pairs={{8,0},{10,2},{12,4},{14,6},{1,9},{3,11},{5,13},{7,15},{24,16},{26,... | collective-permute-start | bytes 393224 | tf_op jit(solution)/shard_map/ppermute | solution.py:19
  157.8 2.2 %copy-start.2 = (f32[8,2,256,256]{3,2,1,0:T(8,128)S(1)}, f32[8,2,256,256]{3,2,1,0:T(8,128)}, u32[]{:S(2)}) copy-start(f32[8,2,256,256]{3,2,1,0:T(8,128)} %copy-done.1) | copy-start | bytes 12582916
